TPU v7x, 32 devices: a whole 2x2x4 slice. The times are simulated.
32 devices in a mesh: ex: 4 (over z), col: 4 (over y, core), lay: 2 (over x).
Axes of the slice: x: 2, y: 2, z: 4, core: 2. Of those that a mesh axis runs over, the one named last changes fastest.
Arguments:
- normalized: bfloat16 [256, 2, 4, 3584], P('ex', 'lay', None, 'col'), may hold values from -6 to 6
- upstream: bfloat16 [256, 2, 4, 3584], P('ex', 'lay', None, 'col'), may hold values from -3 to 3
- owner_order: int32 [4, 64], P('ex'), may hold values from 0 to 63, each once within a row
- sketch_index: int32 [2, 28, 4], P(None, 'col'), may hold values from 0 to 63, all different within a row
- sketch_scale: bfloat16 [2, 28, 4], P(None, 'col'), may hold values from -1.5 to 1.5
- query_sketch: bfloat16 [4, 8192], P('ex', 'col'), may hold values from -0.0625 to 0.0625
Outputs:
- sketch: bfloat16 [256, 8192], P(('ex', 'lay'), 'col')
- scores: float32 [256, 4], P(('ex', 'lay'), 'col')
Inputs may be any that keep to these rules, and one draw needn't show every extreme that they name: Each row is an ordering of the 64 examples of one block; the example at place j of row g is training example g * 64 + owner_order[g, j]. `sketch_index`: the 4 output blocks of one input block are distinct; every output block is named by some input block.
All inputs are finite; a program needn't handle non-finite values.
Results may differ from a plain program's by a relative error of at most 0.0049.
Values may be sent and summed in bfloat16 or wider, within the bound.
A program may use at most 64 MiB of HBM per device.

v0:
```python
import math
import jax
import jax.numpy as jnp
from jax import lax
from jax.sharding import PartitionSpec as P

SKETCH = 8192


def hadamard_table():
    counter = jnp.arange(128, dtype=jnp.int32)
    both = counter[:, None] & counter[None, :]
    parity = jnp.zeros((128, 128), jnp.int32)
    for shift_bit in range(7):
        parity = parity + (both >> shift_bit & 1)
    signs = 1 - 2 * (parity % 2)
    return signs.astype(jnp.float32) / math.sqrt(128.0)


def build_table(sketch_index, sketch_scale, out_blocks):
    targets = jnp.arange(out_blocks, dtype=jnp.int32)
    table = (sketch_index[..., None] == targets).astype(jnp.float32) * sketch_scale.astype(
        jnp.float32
    )[..., None]
    return jnp.sum(table, axis=2).reshape(-1, out_blocks)


def local(normalized, upstream, owner_order, sketch_index, sketch_scale, query_sketch):
    local_grads = jnp.sum(
        normalized.astype(jnp.float32) * upstream.astype(jnp.float32), axis=2
    ).astype(jnp.bfloat16)
    reordered = jnp.take(local_grads, owner_order[0], axis=0)
    owned = lax.all_to_all(reordered, "lay", split_axis=0, concat_axis=1, tiled=True)
    own_rows = owned.shape[0]
    out_blocks = SKETCH // 128
    full_rows, full_index, full_scale = (
        lax.all_gather(owned, "col", axis=2, tiled=True),
        lax.all_gather(sketch_index, "col", axis=1, tiled=True),
        lax.all_gather(sketch_scale, "col", axis=1, tiled=True),
    )
    layer_count, feature_width = (full_rows.shape[1], full_rows.shape[2])
    table = build_table(full_index, full_scale, out_blocks)
    my_blocks = out_blocks // lax.axis_size("col")
    my_table = lax.dynamic_slice_in_dim(table, lax.axis_index("col") * my_blocks, my_blocks, 1)
    grad_rows = full_rows.reshape(own_rows, layer_count * (feature_width // 128), 128).astype(
        jnp.float32
    )
    summed = jnp.einsum("ebc,bo->eoc", grad_rows, my_table, precision=lax.Precision.HIGHEST)
    rotated = jnp.einsum("eoc,cd->eod", summed, hadamard_table(), precision=lax.Precision.HIGHEST)
    sketch = rotated.reshape(own_rows, -1).astype(jnp.bfloat16)
    partial_scores = jnp.einsum(
        "ec,qc->eq",
        sketch,
        lax.all_gather(query_sketch, "ex", axis=0, tiled=True),
        preferred_element_type=jnp.float32,
    )
    scores = lax.psum_scatter(partial_scores, "col", scatter_dimension=1, tiled=True)
    return (sketch, scores)


def solution(mesh):
    placed = (
        P("ex", "lay", None, "col"),
        P("ex", "lay", None, "col"),
        P("ex", None),
        P(None, "col", None),
        P(None, "col", None),
        P("ex", "col"),
    )
    return jax.shard_map(
        local,
        mesh=mesh,
        in_specs=placed,
        out_specs=(P(("ex", "lay"), "col"), P(("ex", "lay"), "col")),
        check_vma=False,
    )
```

profile of v0, /device:TPU:0, one launch (start us, length us, event | category | flops | bytes accessed | tf_op | source)
XLA Modules:
  0.0 53.9 jit_solution(2970445033246631568)
XLA Ops:
  0.6 0.0 copy-start.4
  0.6 0.7 %fusion.23 = s32[64]{0:T(128)S(1)} fusion(s32[1,64]{1,0:T(1,128)} %param.8), kind=kLoop, calls=%fused_computation.37 | loop fusion | flops 192 | bytes 512 | tf_op jit(solution)/shard_map/jit(_take)/jit(_where)/select_n | solution.py:32
  1.4 0.0 copy-done.4
  1.4 1.8 %multiply_reduce_fusion = bf16[64,896]{1,0:T(8,128)(2,1)S(1)} fusion(bf16[64,1,4,896]{3,2,1,0:T(4,128)(2,1)} %param.7, bf16[64,1,4,896]{3,2,1,0:T(4,128)(2,1)} %param.6), kind=kLoop, calls=%fused_computation.3 | loop fusion | flops 860160 | bytes 1032192 | tf_op jit(solution)/shard_map/reduce_sum | solution.py:29
  3.2 0.7 %gather_fusion = bf16[64,896]{1,0:T(8,128)(2,1)S(1)} fusion(bf16[64,896]{1,0:T(8,128)(2,1)S(1)} %multiply_reduce_fusion, s32[1024]{0:T(1024)S(1)} %pad_clamp_fusion), kind=kCustom, calls=%fused_computation | custom fusion | bytes 229632 | tf_op jit(solution)/shard_map/jit(_take)/gather | solution.py:32
  3.9 0.1 bitcast_select_fusion
  4.0 0.5 broadcast.80
  4.6 0.7 %reduce.1 = bf16[64,896]{1,0:T(8,128)(2,1)S(1)} reduce(bf16[64,1,896]{2,0,1:T(8,128)(2,1)S(1)} %bitcast_select_fusion, bf16[]{:T(256)} %broadcast.80), dimensions={1}, to_apply=%copy.40.reduce_sub_computation | reduce | bytes 229378 | tf_op jit(solution)/shard_map/jit(_take)/select_n | solution.py:32
  5.2 0.7 %reshape.102 = bf16[2,2,14336]{2,1,0:T(2,128)(2,1)} reshape(bf16[64,896]{1,0:T(8,128)(2,1)S(1)} %reduce.1) | data formatting | bytes 229376
  5.9 0.0 copy-start.3
  5.9 4.4 %all-to-all-start = ((bf16[2,2,14336]{2,1,0:T(2,128)(2,1)}), bf16[2,2,14336]{2,1,0:T(2,128)(2,1)S(1)}, u32[]{:S(2)}, u32[]{:S(2)}) async-start(bf16[2,2,14336]{2,1,0:T(2,128)(2,1)} %reshape.102), calls=%async_computation | async-start | bytes 229376 | tf_op jit(solution)/shard_map/all_to_all | solution.py:33
  10.3 0.0 copy-done.3
  10.3 0.1 copy.36
  10.4 5.4 %all_gather.13 = bf16[2,28,4]{2,0,1:T(2,128)(2,1)S(1)} all-gather(bf16[2,7,4]{2,0,1:T(2,128)(2,1)S(1)} %copy.36), channel_id=1, replica_groups=mesh['ex'=4,'col'=4,'lay'=2] {'col'}, dimensions={1}, use_global_device_ids=true | all-gather | bytes 560 | tf_op jit(solution)/shard_map/all_gather | solution.py:39
  15.8 0.1 copy.37
  15.9 0.0 copy-start.2
  15.9 0.1 copy.38
  16.0 0.6 %copy-done.2 = s32[2,7,4]{1,2,0:T(4,128)S(1)} copy-done((s32[2,7,4]{1,2,0:T(4,128)S(1)}, s32[2,7,4]{1,2,0:T(4,128)}, u32[]{:S(2)}) %copy-start.2) | copy-done | bytes 248
  16.6 0.1 copy.34
  16.7 5.4 %all_gather.12 = s32[2,28,4]{2,0,1:T(2,128)S(1)} all-gather(s32[2,7,4]{2,0,1:T(2,128)S(1)} %copy.34), channel_id=1, replica_groups=mesh['ex'=4,'col'=4,'lay'=2] {'col'}, dimensions={1}, use_global_device_ids=true | all-gather | bytes 1120 | tf_op jit(solution)/shard_map/all_gather | solution.py:38
  22.1 0.2 select_reduce_fusion
  22.3 0.0 copy-start.1
  22.4 0.0 copy-start.5
  22.4 0.6 %copy-done.5 = u32[32]{0:T(128)S(1)} copy-done((u32[32]{0:T(128)S(1)}, u32[32]{0:T(128)}, u32[]{:S(2)}) %copy-start.5) | copy-done | bytes 152
  23.0 0.7 %dynamic-slice = u32[1]{0:T(128)} dynamic-slice(u32[32]{0:T(128)S(1)} %copy-done.5, u32[]{:T(128)S(6)} %add.63), dynamic_slice_sizes={1} | dynamic-slice | bytes 12
  23.7 0.0 copy-done.1
  23.7 13.5 %all-gather.1 = bf16[4,1,2048]{2,1,0:T(2,128)(2,1)S(1)} all-gather(bf16[1,1,2048]{2,1,0:T(2,128)(2,1)S(1)} %bitcast.38), channel_id=1, replica_groups=mesh['ex'=4,'col'=4,'lay'=2] {'ex'}, dimensions={0}, use_global_device_ids=true | all-gather | bytes 20480 | tf_op jit(solution)/shard_map/all_gather | solution.py:54
  37.2 0.0 all-to-all-done
  37.2 0.1 reshape.103
  37.4 6.8 %all-gather = bf16[32,2,1,3584]{3,0,1,2:T(8,128)(2,1)S(1)} all-gather(bf16[32,2,1,896]{3,0,1,2:T(8,128)(2,1)S(1)} %bitcast.34), channel_id=2, replica_groups=mesh['ex'=4,'col'=4,'lay'=2] {'col'}, dimensions={3}, use_global_device_ids=true | all-gather | bytes 573440 | tf_op jit(solution)/shard_map/all_gather | solution.py:37
  44.2 0.5 copy.41
  44.7 0.3 reshape.83
  45.0 0.5 convolution_bitcast_fusion
  45.4 0.4 convolution_convert_fusion
  45.9 0.0 copy-start
  45.9 0.1 fusion.20
  46.1 6.6 %all-reduce = f32[32,4]{0,1:T(4,128)S(1)} all-reduce(f32[32,4]{0,1:T(4,128)S(1)} %fusion.20), channel_id=3, replica_groups=mesh['ex'=4,'col'=4,'lay'=2] {'col'}, use_global_device_ids=true, to_apply=%region_2.3.clone | all-reduce | flops 128 | bytes 1024
  52.7 1.2 %constant_dynamic-slice_fusion = f32[32,1]{0,1:T(1,128)} fusion(f32[32,4]{0,1:T(4,128)S(1)} %all-reduce, u32[]{:T(128)} %bitcast.9), kind=kLoop, calls=%fused_computation.38 | loop fusion | bytes 260
  53.9 0.0 copy-done
  (6 shorter events, 0.1 us)
Async XLA Ops:
  0.6 0.7 %copy-start.4 = (s32[1,64]{1,0:T(1,128)S(1)}, s32[1,64]{1,0:T(1,128)}, u32[]{:S(2)}) copy-start(s32[1,64]{1,0:T(1,128)} %param.8) | copy-start | bytes 772
  5.9 4.4 %copy-start.3 = (bf16[2,7,4]{1,2,0:T(4,128)(2,1)S(1)}, bf16[2,7,4]{1,2,0:T(4,128)(2,1)}, u32[]{:S(2)}) copy-start(bf16[2,7,4]{1,2,0:T(4,128)(2,1)} %param.10) | copy-start | bytes 340
  5.9 31.3 %all-to-all-start = ((bf16[2,2,14336]{2,1,0:T(2,128)(2,1)}), bf16[2,2,14336]{2,1,0:T(2,128)(2,1)S(1)}, u32[]{:S(2)}, u32[]{:S(2)}) async-start(bf16[2,2,14336]{2,1,0:T(2,128)(2,1)} %reshape.102), calls=%async_computation | async-start | bytes 229376 | tf_op jit(solution)/shard_map/all_to_all | solution.py:33
  15.9 0.7 %copy-start.2 = (s32[2,7,4]{1,2,0:T(4,128)S(1)}, s32[2,7,4]{1,2,0:T(4,128)}, u32[]{:S(2)}) copy-start(s32[2,7,4]{1,2,0:T(4,128)} %param.9) | copy-start | bytes 676
  22.3 1.3 %copy-start.1 = (bf16[1,2048]{1,0:T(2,128)(2,1)S(1)}, bf16[1,2048]{1,0:T(2,128)(2,1)}, u32[]{:S(2)}) copy-start(bf16[1,2048]{1,0:T(2,128)(2,1)} %param.11) | copy-start | bytes 12292
  22.4 0.7 %copy-start.5 = (u32[32]{0:T(128)S(1)}, u32[32]{0:T(128)}, u32[]{:S(2)}) copy-start(u32[32]{0:T(128)} %constant.65) | copy-start | bytes 388
  45.9 7.9 %copy-start = (bf16[4,8,16,128]{3,1,2,0:T(8,128)(2,1)}, bf16[4,8,16,128]{3,1,2,0:T(8,128)(2,1)S(1)}, u32[]{:S(2)}) copy-start(bf16[4,8,16,128]{3,1,2,0:T(8,128)(2,1)S(1)} %copy.51) | copy-start | bytes 393220
where the time goes:
time: 54.3 us; the launch traced here: 53.9 us
  blocking collectives  37.8 us (70%)
  local copies, waits for them, and re-layouts  6.38 us (12%)
  starting transfers between devices  4.37 us (8%)
  other arithmetic  3.53 us (7%)
  matrix products  1.03 us (2%)
  between operations  0.78 us (1%)
    all_gather x1, blocking collectives, local(): lax.all_gather(query_sketch, 'ex', axis=0, tiled=True)  13.5 us
    all_gather x1, blocking collectives, local(): lax.all_gather(owned, 'col', axis=2, tiled=True)  6.84 us
    unnamed x1, blocking collectives  6.58 us
    all_gather x1, blocking collectives, local(): lax.all_gather(sketch_index, 'col', axis=1, tiled=True)  5.43 us
    all_gather x1, blocking collectives, local(): lax.all_gather(sketch_scale, 'col', axis=1, tiled=True)  5.39 us
    all_to_all x1, starting transfers between devices, local(): lax.all_to_all(reordered, 'lay', split_axis=0, concat_axis=1, tiled=True)  4.37 us
    unnamed x20, local copies, waits for them, and re-layouts  4.15 us
    reduce_sum x1, other arithmetic, local(): jnp.sum(normalized.astype(jnp.float32) * upstream.astype(jnp.float32), ax...  1.84 us
  transfers between devices with their start and end apart: 1, of which 0 were waited for; matrix products, arithmetic and copies ran while one was open for 2% of the time, Pallas kernels for 0%

commit v1 on v0

--- a/solution.py
+++ b/solution.py
@@ -48,11 +48,31 @@
     summed = jnp.einsum("ebc,bo->eoc", grad_rows, my_table, precision=lax.Precision.HIGHEST)
     rotated = jnp.einsum("eoc,cd->eod", summed, hadamard_table(), precision=lax.Precision.HIGHEST)
     sketch = rotated.reshape(own_rows, -1).astype(jnp.bfloat16)
+
+    def reach_sectors(v0):
+        a_now = lax.axis_size("ex")
+        front = lax.axis_index("ex")
+        raw_out, last, arr_now = (a_now, front, v0.shape[0])
+        pool = [(q, (q + 1) % raw_out) for q in range(raw_out)]
+        buffers = [(q, (q - 1) % raw_out) for q in range(raw_out)]
+        local_next = jnp.zeros((*v0.shape[:0], raw_out * arr_now, *v0.shape[1:]), v0.dtype)
+        local_next = lax.dynamic_update_slice_in_dim(local_next, v0, last * arr_now, axis=0)
+        shaped = block_next = v0
+        block_last = raw_out // 2
+        for no in range(1, block_last + 1):
+            shaped = lax.ppermute(shaped, "ex", pool)
+            local_next = lax.dynamic_update_slice_in_dim(
+                local_next, shaped, (last - no) % raw_out * arr_now, axis=0
+            )
+            if no < raw_out - block_last:
+                block_next = lax.ppermute(block_next, "ex", buffers)
+                local_next = lax.dynamic_update_slice_in_dim(
+                    local_next, block_next, (last + no) % raw_out * arr_now, axis=0
+                )
+        return local_next
+
     partial_scores = jnp.einsum(
-        "ec,qc->eq",
-        sketch,
-        lax.all_gather(query_sketch, "ex", axis=0, tiled=True),
-        preferred_element_type=jnp.float32,
+        "ec,qc->eq", sketch, reach_sectors(query_sketch), preferred_element_type=jnp.float32
     )
     scores = lax.psum_scatter(partial_scores, "col", scatter_dimension=1, tiled=True)
     return (sketch, scores)

time: 54.3 us -> 48.9 us (0.901)
  blocking collectives: 37.8 us -> 24 us
  starting transfers between devices: 4.37 us -> 8.75 us
  waiting for transfers between devices: 0.01 us -> 3.08 us
  local copies, waits for them, and re-layouts: 6.38 us -> 7.32 us
    all_gather x1 -> x0, blocking collectives: 13.5 us -> none  [local(): lax.all_gather(query_sketch, 'ex', axis=0, tiled=True)]
    ppermute x0 -> x3, starting transfers between devices: none -> 5.26 us  [the longest x2 3.16 us: reach_sectors(): shaped = lax.ppermute(shaped, 'ex', pool)]
    ppermute x0 -> x3, waiting for transfers between devices: none -> 3.08 us  [the longest x2 3.07 us: reach_sectors(): shaped = lax.ppermute(shaped, 'ex', pool)]
    all_to_all x1, starting transfers between devices: 4.37 us -> 3.49 us  [local(): lax.all_to_all(reordered, 'lay', split_axis=0, concat_axis=1, tiled=True)]
    unnamed x20, local copies, waits for them, and re-layouts: 4.15 us -> 4.82 us
  transfers between devices with their start and end apart: 1 -> 4, of which waited for: 0 -> 1; matrix products, arithmetic and copies ran while one was open for 2% -> 14% of each run, Pallas kernels for 0% -> 0%
where the time goes in v1:
time: 48.9 us; the launch traced here: 48.5 us
  blocking collectives  24 us (49%)
  starting transfers between devices  8.75 us (18%)
  local copies, waits for them, and re-layouts  7.32 us (15%)
  other arithmetic  3.46 us (7%)
  waiting for transfers between devices  3.08 us (6%)
  matrix products  1.03 us (2%)
  between operations  0.94 us (2%)
    all_gather x1, blocking collectives, local(): lax.all_gather(owned, 'col', axis=2, tiled=True)  7 us
    unnamed x1, blocking collectives  6.58 us
    all_gather x1, blocking collectives, local(): lax.all_gather(sketch_index, 'col', axis=1, tiled=True)  5.2 us
    all_gather x1, blocking collectives, local(): lax.all_gather(sketch_scale, 'col', axis=1, tiled=True)  5.18 us
    unnamed x20, local copies, waits for them, and re-layouts  4.82 us
    all_to_all x1, starting transfers between devices, local(): lax.all_to_all(reordered, 'lay', split_axis=0, concat_axis=1, tiled=True)  3.49 us
    ppermute x2, starting transfers between devices, reach_sectors(): shaped = lax.ppermute(shaped, 'ex', pool)  3.16 us
    ppermute x2, waiting for transfers between devices, reach_sectors(): shaped = lax.ppermute(shaped, 'ex', pool)  3.07 us
  transfers between devices with their start and end apart: 4, of which 1 were waited for; matrix products, arithmetic and copies ran while one was open for 14% of the time, Pallas kernels for 0%

profile of v1, /device:TPU:0, one launch (start us, length us, event | category | flops | bytes accessed | tf_op | source)
XLA Modules:
  0.0 48.5 jit_solution(7467702039455661082)
XLA Ops:
  0.6 0.0 copy-start.4
  0.6 3.1 %collective-permute-start = (bf16[1,2048]{1,0:T(2,128)(2,1)}, bf16[1,2048]{1,0:T(2,128)(2,1)S(1)}, u32[]{:S(2)}, u32[]{:S(2)}) collective-permute-start(bf16[1,2048]{1,0:T(2,128)(2,1)} %param.11), channel_id=1, source_target_pairs={{0,8},{8,16},{16,24},{24,0},{1,9},{9,17},{17,25},{25,1},{2,10},{10... | collective-permute-start | bytes 12296 | tf_op jit(solution)/shard_map/ppermute | solution.py:63
  3.7 2.1 %collective-permute-start.1 = (bf16[1,2048]{1,0:T(2,128)(2,1)}, bf16[1,2048]{1,0:T(2,128)(2,1)S(1)}, u32[]{:S(2)}, u32[]{:S(2)}) collective-permute-start(bf16[1,2048]{1,0:T(2,128)(2,1)} %param.11), channel_id=1, source_target_pairs={{0,24},{8,0},{16,8},{24,16},{1,25},{9,1},{17,9},{25,17},{2,26},{10... | collective-permute-start | bytes 12296 | tf_op jit(solution)/shard_map/ppermute | solution.py:68
  5.8 0.7 %fusion.20 = s32[64]{0:T(128)S(1)} fusion(s32[1,64]{1,0:T(1,128)} %param.8), kind=kLoop, calls=%fused_computation.34 | loop fusion | flops 192 | bytes 512 | tf_op jit(solution)/shard_map/jit(_take)/jit(_where)/select_n | solution.py:32
  6.5 0.0 copy-done.4
  6.5 1.8 %multiply_reduce_fusion = bf16[64,896]{1,0:T(8,128)(2,1)S(1)} fusion(bf16[64,1,4,896]{3,2,1,0:T(4,128)(2,1)} %param.7, bf16[64,1,4,896]{3,2,1,0:T(4,128)(2,1)} %param.6), kind=kLoop, calls=%fused_computation.3 | loop fusion | flops 860160 | bytes 1032192 | tf_op jit(solution)/shard_map/reduce_sum | solution.py:29
  8.4 0.7 %gather_fusion = bf16[64,896]{1,0:T(8,128)(2,1)S(1)} fusion(bf16[64,896]{1,0:T(8,128)(2,1)S(1)} %multiply_reduce_fusion, s32[1024]{0:T(1024)S(1)} %pad_clamp_fusion), kind=kCustom, calls=%fused_computation | custom fusion | bytes 229632 | tf_op jit(solution)/shard_map/jit(_take)/gather | solution.py:32
  9.1 0.1 bitcast_select_fusion
  9.2 0.5 %broadcast.83 = bf16[]{:T(256)} broadcast(bf16[]{:T(256)} %constant.134), dimensions={} | broadcast | bytes 4 | tf_op jit(solution)/shard_map/jit(_take)/select_n | solution.py:32
  9.7 0.7 %reduce.1 = bf16[64,896]{1,0:T(8,128)(2,1)S(1)} reduce(bf16[64,1,896]{2,0,1:T(8,128)(2,1)S(1)} %bitcast_select_fusion, bf16[]{:T(256)} %broadcast.83), dimensions={1}, to_apply=%copy.40.reduce_sub_computation | reduce | bytes 229378 | tf_op jit(solution)/shard_map/jit(_take)/select_n | solution.py:32
  10.4 0.7 %reshape.100 = bf16[2,2,14336]{2,1,0:T(2,128)(2,1)} reshape(bf16[64,896]{1,0:T(8,128)(2,1)S(1)} %reduce.1) | data formatting | bytes 229376
  11.0 0.0 copy-start.3
  11.0 3.5 %all-to-all-start = ((bf16[2,2,14336]{2,1,0:T(2,128)(2,1)}), bf16[2,2,14336]{2,1,0:T(2,128)(2,1)S(1)}, u32[]{:S(2)}, u32[]{:S(2)}) async-start(bf16[2,2,14336]{2,1,0:T(2,128)(2,1)} %reshape.100), calls=%async_computation | async-start | bytes 229376 | tf_op jit(solution)/shard_map/all_to_all | solution.py:33
  14.5 0.0 copy-done.3
  14.6 0.1 copy.36
  14.7 5.2 %all_gather.10 = bf16[2,28,4]{2,0,1:T(2,128)(2,1)S(1)} all-gather(bf16[2,7,4]{2,0,1:T(2,128)(2,1)S(1)} %copy.36), channel_id=1, replica_groups=mesh['ex'=4,'col'=4,'lay'=2] {'col'}, dimensions={1}, use_global_device_ids=true | all-gather | bytes 560 | tf_op jit(solution)/shard_map/all_gather | solution.py:39
  19.8 0.1 copy.37
  20.0 0.0 copy-start.2
  20.0 0.1 copy.38
  20.1 0.6 %copy-done.2 = s32[2,7,4]{1,2,0:T(4,128)S(1)} copy-done((s32[2,7,4]{1,2,0:T(4,128)S(1)}, s32[2,7,4]{1,2,0:T(4,128)}, u32[]{:S(2)}) %copy-start.2) | copy-done | bytes 248
  20.6 0.1 copy.34
  20.7 5.2 %all_gather.9 = s32[2,28,4]{2,0,1:T(2,128)S(1)} all-gather(s32[2,7,4]{2,0,1:T(2,128)S(1)} %copy.34), channel_id=1, replica_groups=mesh['ex'=4,'col'=4,'lay'=2] {'col'}, dimensions={1}, use_global_device_ids=true | all-gather | bytes 1120 | tf_op jit(solution)/shard_map/all_gather | solution.py:38
  25.9 0.2 select_reduce_fusion
  26.1 0.0 collective-permute-done
  26.2 0.1 collective-permute-start.2
  26.3 0.0 copy-start.1
  26.3 0.7 %copy-done.1 = bf16[1,2048]{1,0:T(2,128)(2,1)S(1)} copy-done((bf16[1,2048]{1,0:T(2,128)(2,1)S(1)}, bf16[1,2048]{1,0:T(2,128)(2,1)}, u32[]{:S(2)}) %copy-start.1) | copy-done | bytes 4120
  27.0 0.1 dynamic_update_slice.12
  27.1 0.0 copy-start.5
  27.1 0.6 %copy-done.5 = u32[32]{0:T(128)S(1)} copy-done((u32[32]{0:T(128)S(1)}, u32[32]{0:T(128)}, u32[]{:S(2)}) %copy-start.5) | copy-done | bytes 152
  27.8 0.7 %dynamic-slice = u32[1]{0:T(128)} dynamic-slice(u32[32]{0:T(128)S(1)} %copy-done.5, u32[]{:T(128)S(6)} %add.98), dynamic_slice_sizes={1} | dynamic-slice | bytes 12
  28.4 0.1 dynamic_update_slice.13
  28.5 0.0 collective-permute-done.1
  28.5 0.1 dynamic_update_slice.14
  28.6 3.1 %collective-permute-done.2 = bf16[1,2048]{1,0:T(2,128)(2,1)S(1)} collective-permute-done((bf16[1,2048]{1,0:T(2,128)(2,1)S(1)}, bf16[1,2048]{1,0:T(2,128)(2,1)S(1)}, u32[]{:S(2)}, u32[]{:S(2)}) %collective-permute-start.2) | collective-permute-done | bytes 4128 | tf_op jit(solution)/shard_map/ppermute | solution.py:63
  31.7 0.1 dynamic_update_slice.15
  31.7 0.0 all-to-all-done
  31.7 0.1 reshape.101
  31.9 7.0 %all-gather = bf16[32,2,1,3584]{3,0,1,2:T(8,128)(2,1)S(1)} all-gather(bf16[32,2,1,896]{3,0,1,2:T(8,128)(2,1)S(1)} %bitcast.31), channel_id=2, replica_groups=mesh['ex'=4,'col'=4,'lay'=2] {'col'}, dimensions={3}, use_global_device_ids=true | all-gather | bytes 573440 | tf_op jit(solution)/shard_map/all_gather | solution.py:37
  38.9 0.5 copy.41
  39.4 0.3 reshape.83
  39.7 0.5 convolution_bitcast_fusion
  40.1 0.4 convolution_convert_fusion
  40.6 0.0 copy-start
  40.6 0.1 fusion.30
  40.8 6.6 %all-reduce = f32[32,4]{0,1:T(4,128)S(1)} all-reduce(f32[32,4]{0,1:T(4,128)S(1)} %fusion.30), channel_id=3, replica_groups=mesh['ex'=4,'col'=4,'lay'=2] {'col'}, use_global_device_ids=true, to_apply=%region_2.3.clone | all-reduce | flops 128 | bytes 1024
  47.3 1.2 %constant_dynamic-slice_fusion = f32[32,1]{0,1:T(1,128)} fusion(f32[32,4]{0,1:T(4,128)S(1)} %all-reduce, u32[]{:T(128)} %bitcast.8), kind=kLoop, calls=%fused_computation.35 | loop fusion | bytes 260
  48.5 0.0 copy-done
  (7 shorter events, 0.1 us)
Async XLA Ops:
  0.6 5.9 %copy-start.4 = (s32[1,64]{1,0:T(1,128)S(1)}, s32[1,64]{1,0:T(1,128)}, u32[]{:S(2)}) copy-start(s32[1,64]{1,0:T(1,128)} %param.8) | copy-start | bytes 772
  0.6 25.5 %collective-permute-start = (bf16[1,2048]{1,0:T(2,128)(2,1)}, bf16[1,2048]{1,0:T(2,128)(2,1)S(1)}, u32[]{:S(2)}, u32[]{:S(2)}) collective-permute-start(bf16[1,2048]{1,0:T(2,128)(2,1)} %param.11), channel_id=1, source_target_pairs={{0,8},{8,16},{16,24},{24,0},{1,9},{9,17},{17,25},{25,1},{2,10},{10... | collective-permute-start | bytes 12296 | tf_op jit(solution)/shard_map/ppermute | solution.py:63
  3.7 24.7 %collective-permute-start.1 = (bf16[1,2048]{1,0:T(2,128)(2,1)}, bf16[1,2048]{1,0:T(2,128)(2,1)S(1)}, u32[]{:S(2)}, u32[]{:S(2)}) collective-permute-start(bf16[1,2048]{1,0:T(2,128)(2,1)} %param.11), channel_id=1, source_target_pairs={{0,24},{8,0},{16,8},{24,16},{1,25},{9,1},{17,9},{25,17},{2,26},{10... | collective-permute-start | bytes 12296 | tf_op jit(solution)/shard_map/ppermute | solution.py:68
  11.0 3.5 %copy-start.3 = (bf16[2,7,4]{1,2,0:T(4,128)(2,1)S(1)}, bf16[2,7,4]{1,2,0:T(4,128)(2,1)}, u32[]{:S(2)}) copy-start(bf16[2,7,4]{1,2,0:T(4,128)(2,1)} %param.10) | copy-start | bytes 340
  11.0 20.7 %all-to-all-start = ((bf16[2,2,14336]{2,1,0:T(2,128)(2,1)}), bf16[2,2,14336]{2,1,0:T(2,128)(2,1)S(1)}, u32[]{:S(2)}, u32[]{:S(2)}) async-start(bf16[2,2,14336]{2,1,0:T(2,128)(2,1)} %reshape.100), calls=%async_computation | async-start | bytes 229376 | tf_op jit(solution)/shard_map/all_to_all | solution.py:33
  20.0 0.7 %copy-start.2 = (s32[2,7,4]{1,2,0:T(4,128)S(1)}, s32[2,7,4]{1,2,0:T(4,128)}, u32[]{:S(2)}) copy-start(s32[2,7,4]{1,2,0:T(4,128)} %param.9) | copy-start | bytes 676
  26.2 5.5 %collective-permute-start.2 = (bf16[1,2048]{1,0:T(2,128)(2,1)S(1)}, bf16[1,2048]{1,0:T(2,128)(2,1)S(1)}, u32[]{:S(2)}, u32[]{:S(2)}) collective-permute-start(bf16[1,2048]{1,0:T(2,128)(2,1)S(1)} %collective-permute-done), channel_id=1, source_target_pairs={{0,8},{8,16},{16,24},{24,0},{1,9},{9,17},{17,25},{25,1},{2,10},{10... | collective-permute-start | bytes 12296 | tf_op jit(solution)/shard_map/ppermute | solution.py:63
  26.3 0.7 %copy-start.1 = (bf16[1,2048]{1,0:T(2,128)(2,1)S(1)}, bf16[1,2048]{1,0:T(2,128)(2,1)}, u32[]{:S(2)}) copy-start(bf16[1,2048]{1,0:T(2,128)(2,1)} %param.11) | copy-start | bytes 12292
  27.1 0.7 %copy-start.5 = (u32[32]{0:T(128)S(1)}, u32[32]{0:T(128)}, u32[]{:S(2)}) copy-start(u32[32]{0:T(128)} %constant.93) | copy-start | bytes 388
  40.6 7.9 %copy-start = (bf16[4,8,16,128]{3,1,2,0:T(8,128)(2,1)}, bf16[4,8,16,128]{3,1,2,0:T(8,128)(2,1)S(1)}, u32[]{:S(2)}) copy-start(bf16[4,8,16,128]{3,1,2,0:T(8,128)(2,1)S(1)} %copy.46) | copy-start | bytes 393220
